TPU v7x, 32 devices: a whole 2x2x4 slice. The times are simulated.
32 devices in a mesh: dp: 8 (over y, x, core), tensor: 4 (over z).
Axes of the slice: x: 2, y: 2, z: 4, core: 2. Of those that a mesh axis runs over, the one named last changes fastest.
Arguments:
- block_in: bfloat16 [8192, 4096], P(('dp', 'tensor')), may hold values from -6 to 6
- out_grad: bfloat16 [8192, 4096], P(('dp', 'tensor')), may hold values from -6 to 6
- segment_ids: int32 [8192], P('dp'), may hold values from 0 to 2, as said below
- positions: int32 [8192], P('dp'), may hold values from 0 to 1023, as said below
- group_token_counts: int32 [8], P('dp'), may hold values from 512 to 1024, as said below
- gain_attn: float32 [4096], replicated, may hold values from 0.1 to 1.9
- w_query: bfloat16 [4096, 4096], P('dp', 'tensor'), may hold values from -0.3125 to 0.3125
- w_key: bfloat16 [4096, 4096], P('dp', 'tensor'), may hold values from -0.3125 to 0.3125
- w_value: bfloat16 [4096, 4096], P('dp', 'tensor'), may hold values from -0.09375 to 0.09375
- w_out: bfloat16 [4096, 4096], P('tensor', 'dp'), may hold values from -0.5 to 0.5
- gain_mlp: float32 [4096], replicated, may hold values from 0.1 to 1.9
- w_gate: bfloat16 [4096, 11008], P('dp', 'tensor'), may hold values from -0.09375 to 0.09375
- w_up: bfloat16 [4096, 11008], P('dp', 'tensor'), may hold values from -0.09375 to 0.09375
- w_down: bfloat16 [11008, 4096], P('tensor', 'dp'), may hold values from -0.0546875 to 0.0546875
Outputs:
- block_out: bfloat16 [8192, 4096], P(('dp', 'tensor'))
- input_grad: bfloat16 [8192, 4096], P(('dp', 'tensor'))
- grad_gain_attn: float32 [4096], replicated
- grad_query: float32 [4096, 4096], P('dp', 'tensor')
- grad_key: float32 [4096, 4096], P('dp', 'tensor')
- grad_value: float32 [4096, 4096], P('dp', 'tensor')
- grad_out: float32 [4096, 4096], P('tensor', 'dp')
- grad_gain_mlp: float32 [4096], replicated
- grad_gate: float32 [4096, 11008], P('dp', 'tensor')
- grad_up: float32 [4096, 11008], P('dp', 'tensor')
- grad_down: float32 [11008, 4096], P('tensor', 'dp')
Inputs may be any that keep to these rules, and one draw needn't show every extreme that they name: `segment_ids`: within each group of 1024 rows segment ids never fall; ids 0 and 1 are the group's sequences (1 may be absent) and 2 marks the rows from group_token_counts of that group on, when there are any. In a group whose live rows number 1024 or more, sequence 0 holds at least 1024 rows; otherwise it holds all live rows. Each segment's positions run 0, 1, 2, ... in row order. In every draw some group is one sequence of all 1024 rows. `group_token_counts`: some group is full in every draw.
All inputs are finite; a program needn't handle non-finite values.
Results may differ from a plain program's by a relative error of at most 0.014.
Values may be sent and summed in bfloat16 or wider, within the bound.
No kernel may reach another device: no remote copies, remote signals or barrier semaphores. Data moves between devices by JAX's collectives and lax.ppermute only.
A program may use at most 448 MiB of HBM per device.

v0:
```python
import jax
import jax.numpy as jnp
from jax import lax
from jax.sharding import PartitionSpec as P

QBLOCKS = 4
HEAD_DIM = 128
EPSILON = 1e-05
ROPE_BASE = 10000.0


def matmul(left, right):
    return jnp.dot(left, right, preferred_element_type=jnp.float32)


def left_t(left, right):
    return lax.dot_general(
        left, right, (((0,), (0,)), ((), ())), preferred_element_type=jnp.float32
    )


def right_t(left, right):
    return lax.dot_general(
        left, right, (((1,), (1,)), ((), ())), preferred_element_type=jnp.float32
    )


def rope_tables(position):
    half_dim = HEAD_DIM // 2
    freq_index = jnp.arange(half_dim).astype(jnp.float32)
    frequency = ROPE_BASE ** (-2.0 * freq_index / HEAD_DIM)
    angles = position.astype(jnp.float32)[:, None] * frequency[None, :]
    cos_tab = jnp.cos(angles)
    sine_tab = jnp.sin(angles)
    return (
        jnp.concatenate([cos_tab, cos_tab], 1)[:, None, :],
        jnp.concatenate([sine_tab, sine_tab], 1)[:, None, :],
    )


def rotate(field):
    half_dim = field.shape[-1] // 2
    return jnp.concatenate([-field[..., half_dim:], field[..., :half_dim]], -1)


def rotate_back(field):
    half_dim = field.shape[-1] // 2
    return jnp.concatenate([field[..., half_dim:], -field[..., :half_dim]], -1)


def apply_rope(field, cos_tab, sine_tab):
    return field * cos_tab + rotate(field) * sine_tab


def undo_rope(field, cos_tab, sine_tab):
    return field * cos_tab + rotate_back(field * sine_tab)


def norm_back(layer_in, row_inverse_scale, norm_weight, normalized_gradient):
    standardized_gradient = normalized_gradient * norm_weight
    standardized_rows = layer_in * row_inverse_scale
    layer_gradient = row_inverse_scale * (
        standardized_gradient
        - standardized_rows
        * jnp.mean(standardized_gradient * standardized_rows, axis=1, keepdims=True)
    )
    return (layer_gradient, jnp.sum(normalized_gradient * standardized_rows, axis=0))


def shards(
    block_in,
    out_grad,
    segment_ids,
    positions,
    group_token_counts,
    gain_attn,
    w_query,
    w_key,
    w_value,
    w_out,
    gain_mlp,
    w_gate,
    w_up,
    w_down,
):
    tok_rows = block_in.shape[0]
    query_all, key_all, value_all, out_all = (
        lax.all_gather(w_query, "dp", axis=0, tiled=True),
        lax.all_gather(w_key, "dp", axis=0, tiled=True),
        lax.all_gather(w_value, "dp", axis=0, tiled=True),
        lax.all_gather(w_out, "dp", axis=1, tiled=True),
    )
    gate_all, up_all, down_all = (
        lax.all_gather(w_gate, "dp", axis=0, tiled=True),
        lax.all_gather(w_up, "dp", axis=0, tiled=True),
        lax.all_gather(w_down, "dp", axis=1, tiled=True),
    )
    x_float = block_in.astype(jnp.float32)
    attn_scale = lax.rsqrt(jnp.mean(x_float * x_float, axis=1, keepdims=True) + EPSILON)
    attn_normed = (x_float * attn_scale * gain_attn).astype(jnp.bfloat16)
    whole_attn = lax.all_gather(attn_normed, "tensor", axis=0, tiled=True)
    group_rows = whole_attn.shape[0]
    local_heads = query_all.shape[1] // HEAD_DIM
    cos_tab, sine_tab = rope_tables(positions)

    def split_heads(field):
        return field.reshape(group_rows, local_heads, HEAD_DIM)

    queries = apply_rope(split_heads(matmul(whole_attn, query_all)), cos_tab, sine_tab).astype(
        jnp.bfloat16
    )
    keys_all = apply_rope(split_heads(matmul(whole_attn, key_all)), cos_tab, sine_tab).astype(
        jnp.bfloat16
    )
    values = split_heads(matmul(whole_attn, value_all)).astype(jnp.bfloat16)
    block_rows = group_rows // QBLOCKS
    row_order = jnp.arange(group_rows)
    score_scale = HEAD_DIM ** (-0.5)

    def block_scores(block_index):
        low_row = block_index * block_rows
        high_row = low_row + block_rows
        scores = (
            jnp.einsum(
                "qhd,khd->hqk",
                queries[low_row:high_row],
                keys_all[:high_row],
                preferred_element_type=jnp.float32,
            )
            * score_scale
        )
        allowed = (segment_ids[low_row:high_row, None] == segment_ids[None, :high_row]) & (
            row_order[None, :high_row] <= row_order[low_row:high_row, None]
        )
        return jnp.where(allowed[None], scores, -1e30)

    attn_parts = []
    total_parts = []
    for block_index in range(QBLOCKS):
        high_row = (block_index + 1) * block_rows
        scores = block_scores(block_index)
        row_max = jnp.max(scores, axis=2, keepdims=True)
        log_total = row_max + jnp.log(jnp.sum(jnp.exp(scores - row_max), axis=2, keepdims=True))
        prob_bf = jnp.exp(scores - log_total).astype(jnp.bfloat16)
        attn_parts.append(
            jnp.einsum(
                "hqk,khd->qhd", prob_bf, values[:high_row], preferred_element_type=jnp.float32
            ).astype(jnp.bfloat16)
        )
        total_parts.append(log_total)
    attn_heads = jnp.concatenate(attn_parts, 0)
    attn = attn_heads.reshape(group_rows, local_heads * HEAD_DIM)
    resid = x_float + lax.psum_scatter(
        matmul(attn, out_all), "tensor", scatter_dimension=0, tiled=True
    )
    mlp_scale = lax.rsqrt(jnp.mean(resid * resid, axis=1, keepdims=True) + EPSILON)
    mlp_normed = (resid * mlp_scale * gain_mlp).astype(jnp.bfloat16)
    whole_mlp = lax.all_gather(mlp_normed, "tensor", axis=0, tiled=True)
    gate_pre = matmul(whole_mlp, gate_all)
    up_pre = matmul(whole_mlp, up_all)
    sigmoid_gate = jax.nn.sigmoid(gate_pre)
    silu_gate = gate_pre * sigmoid_gate
    hidden = (silu_gate * up_pre).astype(jnp.bfloat16)
    block_out = (
        resid
        + lax.psum_scatter(
            matmul(hidden, down_all).astype(jnp.bfloat16), "tensor", scatter_dimension=0, tiled=True
        ).astype(jnp.float32)
    ).astype(jnp.bfloat16)
    first_live = lax.axis_index("tensor") * tok_rows
    live = (first_live + jnp.arange(tok_rows) < group_token_counts[0]).astype(jnp.bfloat16)
    live_grad = out_grad * live[:, None]
    whole_grad = lax.all_gather(live_grad, "tensor", axis=0, tiled=True)
    d_hidden = right_t(whole_grad, down_all)
    grad_down_part = left_t(hidden, whole_grad)
    d_gate = (d_hidden * up_pre * sigmoid_gate * (1.0 + gate_pre * (1.0 - sigmoid_gate))).astype(
        jnp.bfloat16
    )
    d_up = (d_hidden * silu_gate).astype(jnp.bfloat16)
    grad_gate_part = left_t(whole_mlp, d_gate)
    grad_up_part = left_t(whole_mlp, d_up)
    d_norm_mlp = lax.psum_scatter(
        right_t(d_gate, gate_all) + right_t(d_up, up_all), "tensor", scatter_dimension=0, tiled=True
    )
    d_from_mlp, gain_mlp_part = norm_back(resid, mlp_scale, gain_mlp, d_norm_mlp)
    d_resid = live_grad.astype(jnp.float32) + d_from_mlp
    d_resid_b = d_resid.astype(jnp.bfloat16)
    whole_resid = lax.all_gather(d_resid_b, "tensor", axis=0, tiled=True)
    grad_out_part = left_t(attn, whole_resid)
    d_attn = split_heads(right_t(whole_resid, out_all).astype(jnp.bfloat16))
    d_q_parts = []
    d_key_sum = jnp.zeros((group_rows, local_heads, HEAD_DIM), jnp.float32)
    d_value_sum = jnp.zeros((group_rows, local_heads, HEAD_DIM), jnp.float32)
    for block_index in range(QBLOCKS):
        low_row = block_index * block_rows
        high_row = low_row + block_rows
        scores = block_scores(block_index)
        prob_full = jnp.exp(scores - total_parts[block_index])
        dout_rows = d_attn[low_row:high_row]
        row_delta = jnp.sum(
            dout_rows.astype(jnp.float32) * attn_heads[low_row:high_row].astype(jnp.float32), axis=2
        )
        row_delta = jnp.swapaxes(row_delta, 0, 1)[:, :, None]
        d_probs = jnp.einsum(
            "qhd,khd->hqk", dout_rows, values[:high_row], preferred_element_type=jnp.float32
        )
        d_scores = (prob_full * (d_probs - row_delta) * score_scale).astype(jnp.bfloat16)
        d_value_sum = d_value_sum.at[:high_row].add(
            jnp.einsum(
                "hqk,qhd->khd",
                prob_full.astype(jnp.bfloat16),
                dout_rows,
                preferred_element_type=jnp.float32,
            )
        )
        d_q_parts.append(
            jnp.einsum(
                "hqk,khd->qhd", d_scores, keys_all[:high_row], preferred_element_type=jnp.float32
            )
        )
        d_key_sum = d_key_sum.at[:high_row].add(
            jnp.einsum(
                "hqk,qhd->khd",
                d_scores,
                queries[low_row:high_row],
                preferred_element_type=jnp.float32,
            )
        )
    local_width = local_heads * HEAD_DIM
    d_queries = (
        undo_rope(jnp.concatenate(d_q_parts, 0), cos_tab, sine_tab)
        .astype(jnp.bfloat16)
        .reshape(group_rows, local_width)
    )
    d_keys = (
        undo_rope(d_key_sum, cos_tab, sine_tab)
        .astype(jnp.bfloat16)
        .reshape(group_rows, local_width)
    )
    d_values = d_value_sum.astype(jnp.bfloat16).reshape(group_rows, local_width)
    grad_query_part = left_t(whole_attn, d_queries)
    grad_key_part = left_t(whole_attn, d_keys)
    grad_value_part = left_t(whole_attn, d_values)
    d_norm_attn = lax.psum_scatter(
        right_t(d_queries, query_all) + right_t(d_keys, key_all) + right_t(d_values, value_all),
        "tensor",
        scatter_dimension=0,
        tiled=True,
    )
    d_from_attn, gain_attn_part = norm_back(x_float, attn_scale, gain_attn, d_norm_attn)
    input_grad = (d_resid + d_from_attn).astype(jnp.bfloat16)
    grad_query, grad_key, grad_value, grad_out, grad_gate, grad_up, grad_down = (
        lax.psum_scatter(grad_query_part, "dp", scatter_dimension=0, tiled=True),
        lax.psum_scatter(grad_key_part, "dp", scatter_dimension=0, tiled=True),
        lax.psum_scatter(grad_value_part, "dp", scatter_dimension=0, tiled=True),
        lax.psum_scatter(grad_out_part, "dp", scatter_dimension=1, tiled=True),
        lax.psum_scatter(grad_gate_part, "dp", scatter_dimension=0, tiled=True),
        lax.psum_scatter(grad_up_part, "dp", scatter_dimension=0, tiled=True),
        lax.psum_scatter(grad_down_part, "dp", scatter_dimension=1, tiled=True),
    )
    grad_gain_attn, grad_gain_mlp = lax.psum((gain_attn_part, gain_mlp_part), ("dp", "tensor"))
    return (
        block_out,
        input_grad,
        grad_gain_attn,
        grad_query,
        grad_key,
        grad_value,
        grad_out,
        grad_gain_mlp,
        grad_gate,
        grad_up,
        grad_down,
    )


def solution(mesh):
    placed = (
        P(("dp", "tensor"), None),
        P(("dp", "tensor"), None),
        P("dp"),
        P("dp"),
        P("dp"),
        P(),
        P("dp", "tensor"),
        P("dp", "tensor"),
        P("dp", "tensor"),
        P("tensor", "dp"),
        P(),
        P("dp", "tensor"),
        P("dp", "tensor"),
        P("tensor", "dp"),
    )
    return jax.shard_map(
        shards,
        mesh=mesh,
        in_specs=placed,
        out_specs=(
            P(("dp", "tensor"), None),
            P(("dp", "tensor"), None),
            P(),
            P("dp", "tensor"),
            P("dp", "tensor"),
            P("dp", "tensor"),
            P("tensor", "dp"),
            P(),
            P("dp", "tensor"),
            P("dp", "tensor"),
            P("tensor", "dp"),
        ),
        check_vma=False,
    )
```

profile of v0, /device:TPU:0, one launch (start us, length us, event | category | flops | bytes accessed | tf_op | source)
XLA Modules:
  0.0 3740.4 jit_solution(11734040073000018754)
XLA Ops:
  22.3 143.7 %all-gather.12.cloned.1.call-done = bf16[1024,4096]{1,0:T(8,128)(2,1)} async-done(((bf16[256,4096]{1,0:T(8,128)(2,1)}), bf16[1024,4096]{1,0:T(8,128)(2,1)}) %all-gather.12.cloned.1.call-update) | async-done | bytes 8388624 | tf_op jit(solution)/shard_map/all_gather | solution.py:101
  166.0 54.5 %all-gather.14.cloned.1.call-done = bf16[4096,1024]{1,0:T(8,128)(2,1)} async-done(((bf16[512,1024]{1,0:T(8,128)(2,1)}), bf16[4096,1024]{1,0:T(8,128)(2,1)}) %all-gather.14.cloned.1.call-update) | async-done | bytes 8388624 | tf_op jit(solution)/shard_map/all_gather | solution.py:90
  237.1 39.7 %all-gather.16.cloned.1.call-done = bf16[4096,1024]{1,0:T(8,128)(2,1)} async-done(((bf16[512,1024]{1,0:T(8,128)(2,1)}), bf16[4096,1024]{1,0:T(8,128)(2,1)}) %all-gather.16.cloned.1.call-update) | async-done | bytes 8388624 | tf_op jit(solution)/shard_map/all_gather | solution.py:88
  297.2 35.8 all-gather.18.cloned.1.call-done
  406.3 279.6 %reduce-scatter.12.cloned.1.call-done = f32[256,4096]{1,0:T(8,128)} async-done(((f32[1024,4096]{1,0:T(8,128)}), f32[256,4096]{1,0:T(8,128)}) %reduce-scatter.12.cloned.1.call-update) | async-done | bytes 4194320 | tf_op jit(solution)/shard_map/reduce_scatter | solution.py:153
  697.1 110.3 %all-gather.24.cloned.1.call-done = bf16[4096,2752]{0,1:T(8,128)(2,1)} async-done(((bf16[512,2752]{0,1:T(8,128)(2,1)}), bf16[4096,2752]{0,1:T(8,128)(2,1)}) %all-gather.24.cloned.1.call-update) | async-done | bytes 22544400 | tf_op jit(solution)/shard_map/all_gather | solution.py:94
  807.4 151.9 %all-gather.22.cloned.1.call-done = bf16[1024,4096]{1,0:T(8,128)(2,1)} async-done(((bf16[256,4096]{1,0:T(8,128)(2,1)}), bf16[1024,4096]{1,0:T(8,128)(2,1)}) %all-gather.22.cloned.1.call-update) | async-done | bytes 8388624 | tf_op jit(solution)/shard_map/all_gather | solution.py:158
  990.1 88.2 %all-gather.26.cloned.1.call-done = bf16[4096,2752]{0,1:T(8,128)(2,1)} async-done(((bf16[512,2752]{0,1:T(8,128)(2,1)}), bf16[4096,2752]{0,1:T(8,128)(2,1)}) %all-gather.26.cloned.1.call-update) | async-done | bytes 22544400 | tf_op jit(solution)/shard_map/all_gather | solution.py:95
  1108.9 121.1 %all-gather.30.cloned.1.call-done = bf16[1024,4096]{1,0:T(8,128)(2,1)} async-done(((bf16[256,4096]{1,0:T(8,128)(2,1)}), bf16[1024,4096]{1,0:T(8,128)(2,1)}) %all-gather.30.cloned.1.call-update) | async-done | bytes 8388624 | tf_op jit(solution)/shard_map/all_gather | solution.py:173
  1230.0 119.0 %all-gather.28.cloned.1.call-done = bf16[2752,4096]{1,0:T(8,128)(2,1)} async-done(((bf16[2752,512]{1,0:T(8,128)(2,1)}), bf16[2752,4096]{1,0:T(8,128)(2,1)}) %all-gather.28.cloned.1.call-update) | async-done | bytes 22544400 | tf_op jit(solution)/shard_map/all_gather | solution.py:96
  1349.0 38.0 %multiply_convert_fusion = (bf16[1024,2752]{0,1:T(8,128)(2,1)}, bf16[1024,2752]{0,1:T(8,128)(2,1)}, bf16[1024,2752]{0,1:T(8,128)(2,1)}) fusion(f32[1024,2752]{0,1:T(8,128)} %fusion.75, f32[1024,2752]{0,1:T(8,128)} %fusion.76, bf16[1024,4096]{1,0:T(8,128)(2,1)} %all-gather.30.cloned.1.call-done, bf16[2752,4096]{1,0:T(8,128)(2,1)} %all-gather.28.cloned.1.call-done), kind=kOutput, calls=%fused_computation.1 | convolution fusion | flops 23127719936 | bytes 70385664 | tf_op jit(solution)/shard_map/dot_general | solution.py:23
  1417.1 32.0 convolution_add_fusion
  1449.2 280.4 %reduce-scatter.16.cloned.1.call-done = f32[256,4096]{1,0:T(8,128)} async-done(((f32[1024,4096]{1,0:T(8,128)}), f32[256,4096]{1,0:T(8,128)}) %reduce-scatter.16.cloned.1.call-update) | async-done | bytes 4194320 | tf_op jit(solution)/shard_map/reduce_scatter | solution.py:182
  1739.5 149.5 %all-gather.32.cloned.1.call-done = bf16[1024,4096]{1,0:T(8,128)(2,1)} async-done(((bf16[256,4096]{1,0:T(8,128)(2,1)}), bf16[1024,4096]{1,0:T(8,128)(2,1)}) %all-gather.32.cloned.1.call-update) | async-done | bytes 8388624 | tf_op jit(solution)/shard_map/all_gather | solution.py:188
  2225.0 86.5 %reduce-scatter.18.cloned.1.call-done = f32[256,4096]{1,0:T(8,128)} async-done(((f32[1024,4096]{1,0:T(8,128)}), f32[256,4096]{1,0:T(8,128)}) %reduce-scatter.18.cloned.1.call-update) | async-done | bytes 4194320 | tf_op jit(solution)/shard_map/reduce_scatter | solution.py:244
  2314.9 46.8 %all-reduce.2 = (f32[4096]{0:T(1024)}, f32[4096]{0:T(1024)}) all-reduce(f32[4096]{0:T(1024)S(1)} %get-tuple-element.125, f32[4096]{0:T(1024)S(1)} %copy-done.65), channel_id=1, replica_groups=mesh['dp'=8,'tensor'=4] {'dp','tensor'}, use_global_device_ids=true, to_apply=%region_21.22 | all-reduce | flops 8192 | bytes 65536 | tf_op jit(solution)/shard_map/psum | solution.py:261
  2361.7 98.3 %reduce-scatter.14.cloned.1.call-done = bf16[256,4096]{1,0:T(8,128)(2,1)} async-done(((bf16[1024,4096]{1,0:T(8,128)(2,1)}), bf16[256,4096]{1,0:T(8,128)(2,1)}) %reduce-scatter.14.cloned.1.call-update) | async-done | bytes 2097168 | tf_op jit(solution)/shard_map/reduce_scatter | solution.py:166
  2468.7 255.4 %reduce-scatter.28.cloned.1.call-done = f32[512,2752]{0,1:T(8,128)} async-done(((f32[4096,2752]{0,1:T(8,128)}), f32[512,2752]{0,1:T(8,128)}) %reduce-scatter.28.cloned.1.call-update) | async-done | bytes 5636112 | tf_op jit(solution)/shard_map/reduce_scatter | solution.py:257
  2724.1 263.4 %reduce-scatter.30.cloned.1.call-done = f32[512,2752]{0,1:T(8,128)} async-done(((f32[4096,2752]{0,1:T(8,128)}), f32[512,2752]{0,1:T(8,128)}) %reduce-scatter.30.cloned.1.call-update) | async-done | bytes 5636112 | tf_op jit(solution)/shard_map/reduce_scatter | solution.py:258
  2987.5 263.5 %reduce-scatter.32.cloned.1.call-done = f32[2752,512]{1,0:T(8,128)} async-done(((f32[2752,4096]{1,0:T(8,128)}), f32[2752,512]{1,0:T(8,128)}) %reduce-scatter.32.cloned.1.call-update) | async-done | bytes 5636112 | tf_op jit(solution)/shard_map/reduce_scatter | solution.py:259
  3251.0 120.6 %reduce-scatter.24.cloned.1.call-done = f32[512,1024]{1,0:T(8,128)} async-done(((f32[4096,1024]{1,0:T(8,128)}), f32[512,1024]{1,0:T(8,128)}) %reduce-scatter.24.cloned.1.call-update) | async-done | bytes 2097168 | tf_op jit(solution)/shard_map/reduce_scatter | solution.py:255
  3371.6 120.4 %reduce-scatter.22.cloned.1.call-done = f32[512,1024]{1,0:T(8,128)} async-done(((f32[4096,1024]{1,0:T(8,128)}), f32[512,1024]{1,0:T(8,128)}) %reduce-scatter.22.cloned.1.call-update) | async-done | bytes 2097168 | tf_op jit(solution)/shard_map/reduce_scatter | solution.py:254
  3492.0 120.6 %reduce-scatter.26.cloned.1.call-done = f32[1024,512]{1,0:T(8,128)} async-done(((f32[1024,4096]{1,0:T(8,128)}), f32[1024,512]{1,0:T(8,128)}) %reduce-scatter.26.cloned.1.call-update) | async-done | bytes 2097168 | tf_op jit(solution)/shard_map/reduce_scatter | solution.py:256
  3612.5 120.6 %reduce-scatter.20.cloned.1.call-done = f32[512,1024]{1,0:T(8,128)} async-done(((f32[4096,1024]{1,0:T(8,128)}), f32[512,1024]{1,0:T(8,128)}) %reduce-scatter.20.cloned.1.call-update) | async-done | bytes 2097168 | tf_op jit(solution)/shard_map/reduce_scatter | solution.py:253
  (335 shorter events, 584.1 us)
Async XLA Ops:
  7.2 158.8 %all-gather.12.cloned.1.call-start = ((), (), s32[]{:S(2)}) async-start(), calls=%async_computation.11 | async-start | bytes 10485760 | tf_op jit(solution)/shard_map/all_gather | solution.py:101
  13.5 207.0 %all-gather.14.cloned.1.call-start = ((), (), s32[]{:S(2)}) async-start(), calls=%async_computation.12 | async-start | bytes 9437184 | tf_op jit(solution)/shard_map/all_gather | solution.py:90
  14.2 262.6 %all-gather.16.cloned.1.call-start = ((), (), s32[]{:S(2)}) async-start(), calls=%async_computation.13 | async-start | bytes 9437184 | tf_op jit(solution)/shard_map/all_gather | solution.py:88
  15.0 318.0 %all-gather.18.cloned.1.call-start = ((), (), s32[]{:S(2)}) async-start(), calls=%async_computation.14 | async-start | bytes 9437184 | tf_op jit(solution)/shard_map/all_gather | solution.py:89
  15.5 375.2 %all-gather.20.cloned.1.call-start = ((), (), s32[]{:S(2)}) async-start(), calls=%async_computation.15 | async-start | bytes 9437184 | tf_op jit(solution)/shard_map/all_gather | solution.py:91
  16.1 669.8 %reduce-scatter.12.cloned.1.call-start = ((), (), s32[]{:S(2)}) async-start(), calls=%async_computation.16 | async-start | bytes 20971520 | tf_op jit(solution)/shard_map/reduce_scatter | solution.py:153
  20.2 341.8 %copy-start.20 = (f32[1024,128]{1,0:T(8,128)}, f32[1024,128]{1,0:T(8,128)S(1)}, u32[]{:S(2)}) copy-start(f32[1024,128]{1,0:T(8,128)S(1)} %get-tuple-element.171) | copy-start | bytes 1572868
  20.2 341.8 %copy-start.30 = (f32[1024,128]{1,0:T(8,128)}, f32[1024,128]{1,0:T(8,128)S(1)}, u32[]{:S(2)}) copy-start(f32[1024,128]{1,0:T(8,128)S(1)} %get-tuple-element.172) | copy-start | bytes 1572868
  405.5 401.9 %all-gather.24.cloned.1.call-start = ((), (), s32[]{:S(2)}) async-start(), calls=%async_computation.18 | async-start | bytes 25362432 | tf_op jit(solution)/shard_map/all_gather | solution.py:94
  406.3 553.0 %all-gather.22.cloned.1.call-start = ((), (), s32[]{:S(2)}) async-start(), calls=%async_computation.17 | async-start | bytes 10485760 | tf_op jit(solution)/shard_map/all_gather | solution.py:158
  692.7 385.6 %all-gather.26.cloned.1.call-start = ((), (), s32[]{:S(2)}) async-start(), calls=%async_computation.19 | async-start | bytes 25362432 | tf_op jit(solution)/shard_map/all_gather | solution.py:95
  693.4 536.6 %all-gather.30.cloned.1.call-start = ((), (), s32[]{:S(2)}) async-start(), calls=%async_computation.22 | async-start | bytes 10485760 | tf_op jit(solution)/shard_map/all_gather | solution.py:173
  696.3 652.7 %all-gather.28.cloned.1.call-start = ((), (), s32[]{:S(2)}) async-start(), calls=%async_computation.20 | async-start | bytes 25362432 | tf_op jit(solution)/shard_map/all_gather | solution.py:96
  697.0 1032.6 %reduce-scatter.16.cloned.1.call-start = ((), (), s32[]{:S(2)}) async-start(), calls=%async_computation.23 | async-start | bytes 20971520 | tf_op jit(solution)/shard_map/reduce_scatter | solution.py:182
  1449.2 439.8 %all-gather.32.cloned.1.call-start = ((), (), s32[]{:S(2)}) async-start(), calls=%async_computation.24 | async-start | bytes 10485760 | tf_op jit(solution)/shard_map/all_gather | solution.py:188
  1738.5 573.0 %reduce-scatter.18.cloned.1.call-start = ((), (), s32[]{:S(2)}) async-start(), calls=%async_computation.25 | async-start | bytes 20971520 | tf_op jit(solution)/shard_map/reduce_scatter | solution.py:244
  2032.8 427.2 %reduce-scatter.14.cloned.1.call-start = ((), (), s32[]{:S(2)}) async-start(), calls=%async_computation.21 | async-start | bytes 10485760 | tf_op jit(solution)/shard_map/reduce_scatter | solution.py:166
  2064.4 659.7 %reduce-scatter.28.cloned.1.call-start = ((), (), s32[]{:S(2)}) async-start(), calls=%async_computation.30 | async-start | bytes 50724864 | tf_op jit(solution)/shard_map/reduce_scatter | solution.py:257
  2096.1 891.5 %reduce-scatter.30.cloned.1.call-start = ((), (), s32[]{:S(2)}) async-start(), calls=%async_computation.31 | async-start | bytes 50724864 | tf_op jit(solution)/shard_map/reduce_scatter | solution.py:258
  2128.0 1123.0 %reduce-scatter.32.cloned.1.call-start = ((), (), s32[]{:S(2)}) async-start(), calls=%async_computation.32 | async-start | bytes 50724864 | tf_op jit(solution)/shard_map/reduce_scatter | solution.py:259
  2159.7 1211.9 %reduce-scatter.24.cloned.1.call-start = ((), (), s32[]{:S(2)}) async-start(), calls=%async_computation.28 | async-start | bytes 18874368 | tf_op jit(solution)/shard_map/reduce_scatter | solution.py:255
  2176.1 1315.9 %reduce-scatter.22.cloned.1.call-start = ((), (), s32[]{:S(2)}) async-start(), calls=%async_computation.27 | async-start | bytes 18874368 | tf_op jit(solution)/shard_map/reduce_scatter | solution.py:254
  2192.4 1420.2 %reduce-scatter.26.cloned.1.call-start = ((), (), s32[]{:S(2)}) async-start(), calls=%async_computation.29 | async-start | bytes 18874368 | tf_op jit(solution)/shard_map/reduce_scatter | solution.py:256
  2208.7 1524.4 %reduce-scatter.20.cloned.1.call-start = ((), (), s32[]{:S(2)}) async-start(), calls=%async_computation.26 | async-start | bytes 18874368 | tf_op jit(solution)/shard_map/reduce_scatter | solution.py:253
  (88 other events, 3409.0 us)
Sparse Core Ops, SparseCore 0:
  13.6 152.3 all-gather.11
  167.8 52.6 all-gather.13
  222.4 54.3 all-gather.15
  278.6 54.3 all-gather.17
  334.7 55.9 all-gather.19
  405.6 280.2 reduce-scatter.11
  688.0 119.3 all-gather.23
  809.6 149.6 all-gather.21
  961.3 116.8 all-gather.25
  1080.3 149.6 all-gather.29
  1232.0 116.8 all-gather.27
  1449.3 280.2 reduce-scatter.15
  1738.6 150.3 all-gather.31
  2032.9 278.5 reduce-scatter.17
  2313.8 146.1 reduce-scatter.13
  2464.6 259.4 reduce-scatter.27
  2728.7 258.7 reduce-scatter.29
  2992.2 258.7 reduce-scatter.31
  3255.6 115.9 reduce-scatter.23
  3376.0 115.9 reduce-scatter.21
  3496.5 115.9 reduce-scatter.25
  3617.1 115.9 reduce-scatter.19
where the time goes:
time: 3750 us; the launch traced here: 3740 us
  waiting for transfers between devices  3030 us (81%)
  matrix products  521 us (14%)
  other arithmetic  75.1 us (2%)
  local copies, waits for them, and re-layouts  50.8 us (1%)
  blocking collectives  46.8 us (1%)
    reduce_scatter x1, waiting for transfers between devices, shards(): lax.psum_scatter(right_t(d_gate, gate_all) + right_t(d_up, up_all), 'tens...  280 us
    reduce_scatter x1, waiting for transfers between devices, shards(): lax.psum_scatter(matmul(attn, out_all), 'tensor', scatter_dimension=0, ti...  280 us
    reduce_scatter x1, waiting for transfers between devices, shards(): lax.psum_scatter(grad_down_part, 'dp', scatter_dimension=1, tiled=True)  263 us
    reduce_scatter x1, waiting for transfers between devices, shards(): lax.psum_scatter(grad_up_part, 'dp', scatter_dimension=0, tiled=True)  263 us
    reduce_scatter x1, waiting for transfers between devices, shards(): lax.psum_scatter(grad_gate_part, 'dp', scatter_dimension=0, tiled=True)  255 us
    dot_general x7, matrix products, right_t(): lax.dot_general(left, right, (((1,), (1,)), ((), ())), preferred_element_...  166 us
    dot_general x7, matrix products, left_t(): lax.dot_general(left, right, (((0,), (0,)), ((), ())), preferred_element_...  154 us
    dot_general x7, matrix products, matmul(): return jnp.dot(left, right, preferred_element_type=jnp.float32)  152 us
  transfers between devices with their start and end apart: 22, of which 22 were waited for; matrix products, arithmetic and copies ran while one was open for 10% of the time, Pallas kernels for 0%

commit v1 on v0

--- a/solution.py
+++ b/solution.py
@@ -170,7 +170,15 @@
     first_live = lax.axis_index("tensor") * tok_rows
     live = (first_live + jnp.arange(tok_rows) < group_token_counts[0]).astype(jnp.bfloat16)
     live_grad = out_grad * live[:, None]
-    whole_grad = lax.all_gather(live_grad, "tensor", axis=0, tiled=True)
+    size = lax.axis_size("tensor")
+    moving, tiles = (live_grad, [live_grad])
+    for _ in range(size - 1):
+        moving = lax.ppermute(moving, "tensor", [(i, (i + 1) % size) for i in range(size)])
+        tiles.insert(0, moving)
+    row_of_blocks = jnp.concatenate(tiles, axis=0)
+    whole_grad = jnp.roll(
+        row_of_blocks, (lax.axis_index("tensor") + 1) * live_grad.shape[0], axis=0
+    )
     d_hidden = right_t(whole_grad, down_all)
     grad_down_part = left_t(hidden, whole_grad)
     d_gate = (d_hidden * up_pre * sigmoid_gate * (1.0 + gate_pre * (1.0 - sigmoid_gate))).astype(

time: 3750 us -> 3630 us (0.968)
  waiting for transfers between devices: 3030 us -> 2880 us
    ppermute x0 -> x3, waiting for transfers between devices: none -> 165 us  [shards(): lax.ppermute(moving, 'tensor', [(i, (i + 1) % size) for i in range(size)])]
    all_gather x1 -> x0, waiting for transfers between devices: 121 us -> none  [shards(): whole_grad = lax.all_gather(live_grad, 'tensor', axis=0, tiled=True)]
    all_gather x1, waiting for transfers between devices: 110 us -> 0.01 us  [shards(): lax.all_gather(w_gate, 'dp', axis=0, tiled=True)]
    all_gather x1, waiting for transfers between devices: 152 us -> 95.4 us  [shards(): whole_mlp = lax.all_gather(mlp_normed, 'tensor', axis=0, tiled=True)]
  transfers between devices with their start and end apart: 22 -> 24, of which waited for: 22 -> 23; matrix products, arithmetic and copies ran while one was open for 10% -> 11% of each run, Pallas kernels for 0% -> 0%
where the time goes in v1:
time: 3630 us; the launch traced here: 3620 us
  waiting for transfers between devices  2880 us (79%)
  matrix products  533 us (15%)
  other arithmetic  76.6 us (2%)
  local copies, waits for them, and re-layouts  70.5 us (2%)
  blocking collectives  46.8 us (1%)
    reduce_scatter x1, waiting for transfers between devices, shards(): lax.psum_scatter(right_t(d_gate, gate_all) + right_t(d_up, up_all), 'tens...  280 us
    reduce_scatter x1, waiting for transfers between devices, shards(): lax.psum_scatter(matmul(attn, out_all), 'tensor', scatter_dimension=0, ti...  280 us
    reduce_scatter x1, waiting for transfers between devices, shards(): lax.psum_scatter(grad_up_part, 'dp', scatter_dimension=0, tiled=True)  263 us
    reduce_scatter x1, waiting for transfers between devices, shards(): lax.psum_scatter(grad_down_part, 'dp', scatter_dimension=1, tiled=True)  263 us
    reduce_scatter x1, waiting for transfers between devices, shards(): lax.psum_scatter(grad_gate_part, 'dp', scatter_dimension=0, tiled=True)  255 us
    dot_general x7, matrix products, right_t(): lax.dot_general(left, right, (((1,), (1,)), ((), ())), preferred_element_...  166 us
    ppermute x3, waiting for transfers between devices, shards(): lax.ppermute(moving, 'tensor', [(i, (i + 1) % size) for i in range(size)])  165 us
    dot_general x7, matrix products, left_t(): lax.dot_general(left, right, (((0,), (0,)), ((), ())), preferred_element_...  154 us
  transfers between devices with their start and end apart: 24, of which 23 were waited for; matrix products, arithmetic and copies ran while one was open for 11% of the time, Pallas kernels for 0%

profile of v1, /device:TPU:0, one launch (start us, length us, event | category | flops | bytes accessed | tf_op | source)
XLA Modules:
  0.0 3621.6 jit_solution(9737265911925905987)
XLA Ops:
  22.3 143.6 %all-gather.11.cloned.1.call-done = bf16[1024,4096]{1,0:T(8,128)(2,1)} async-done(((bf16[256,4096]{1,0:T(8,128)(2,1)}), bf16[1024,4096]{1,0:T(8,128)(2,1)}) %all-gather.11.cloned.1.call-update) | async-done | bytes 8388624 | tf_op jit(solution)/shard_map/all_gather | solution.py:101
  166.0 54.5 %all-gather.13.cloned.1.call-done = bf16[4096,1024]{1,0:T(8,128)(2,1)} async-done(((bf16[512,1024]{1,0:T(8,128)(2,1)}), bf16[4096,1024]{1,0:T(8,128)(2,1)}) %all-gather.13.cloned.1.call-update) | async-done | bytes 8388624 | tf_op jit(solution)/shard_map/all_gather | solution.py:90
  237.5 39.3 %all-gather.15.cloned.1.call-done = bf16[4096,1024]{1,0:T(8,128)(2,1)} async-done(((bf16[512,1024]{1,0:T(8,128)(2,1)}), bf16[4096,1024]{1,0:T(8,128)(2,1)}) %all-gather.15.cloned.1.call-update) | async-done | bytes 8388624 | tf_op jit(solution)/shard_map/all_gather | solution.py:88
  297.2 35.8 all-gather.17.cloned.1.call-done
  406.4 279.7 %reduce-scatter.12.cloned.1.call-done = f32[256,4096]{1,0:T(8,128)} async-done(((f32[1024,4096]{1,0:T(8,128)}), f32[256,4096]{1,0:T(8,128)}) %reduce-scatter.12.cloned.1.call-update) | async-done | bytes 4194320 | tf_op jit(solution)/shard_map/reduce_scatter | solution.py:153
  695.1 49.0 %collective-permute-done = bf16[256,4096]{1,0:T(8,128)(2,1)S(1)} collective-permute-done((bf16[256,4096]{1,0:T(8,128)(2,1)S(1)}, bf16[256,4096]{1,0:T(8,128)(2,1)S(1)}, u32[]{:S(2)}, u32[]{:S(2)}) %collective-permute-start) | collective-permute-done | bytes 2097184 | tf_op jit(solution)/shard_map/ppermute | solution.py:176
  745.5 48.2 %collective-permute-done.1 = bf16[256,4096]{1,0:T(8,128)(2,1)} collective-permute-done((bf16[256,4096]{1,0:T(8,128)(2,1)S(1)}, bf16[256,4096]{1,0:T(8,128)(2,1)}, u32[]{:S(2)}, u32[]{:S(2)}) %collective-permute-start.1) | collective-permute-done | bytes 2097184 | tf_op jit(solution)/shard_map/ppermute | solution.py:176
  793.7 68.0 %collective-permute-done.2 = bf16[256,4096]{1,0:T(8,128)(2,1)} collective-permute-done((bf16[256,4096]{1,0:T(8,128)(2,1)}, bf16[256,4096]{1,0:T(8,128)(2,1)}, u32[]{:S(2)}, u32[]{:S(2)}) %collective-permute-start.2) | collective-permute-done | bytes 2097184 | tf_op jit(solution)/shard_map/ppermute | solution.py:176
  881.3 95.4 %all-gather.21.cloned.1.call-done = bf16[1024,4096]{1,0:T(8,128)(2,1)} async-done(((bf16[256,4096]{1,0:T(8,128)(2,1)}), bf16[1024,4096]{1,0:T(8,128)(2,1)}) %all-gather.21.cloned.1.call-update) | async-done | bytes 8388624 | tf_op jit(solution)/shard_map/all_gather | solution.py:158
  1007.9 87.7 %all-gather.25.cloned.1.call-done = bf16[4096,2752]{0,1:T(8,128)(2,1)} async-done(((bf16[512,2752]{0,1:T(8,128)(2,1)}), bf16[4096,2752]{0,1:T(8,128)(2,1)}) %all-gather.25.cloned.1.call-update) | async-done | bytes 22544400 | tf_op jit(solution)/shard_map/all_gather | solution.py:95
  1126.3 89.9 %all-gather.27.cloned.1.call-done = bf16[2752,4096]{1,0:T(8,128)(2,1)} async-done(((bf16[2752,512]{1,0:T(8,128)(2,1)}), bf16[2752,4096]{1,0:T(8,128)(2,1)}) %all-gather.27.cloned.1.call-update) | async-done | bytes 22544400 | tf_op jit(solution)/shard_map/all_gather | solution.py:96
  1216.2 37.7 %multiply_convert_fusion = (bf16[1024,2752]{0,1:T(8,128)(2,1)}, bf16[1024,2752]{0,1:T(8,128)(2,1)}, bf16[1024,2752]{0,1:T(8,128)(2,1)}) fusion(f32[1024,2752]{0,1:T(8,128)} %fusion.81, f32[1024,2752]{0,1:T(8,128)} %fusion.82, bf16[2752,4096]{1,0:T(8,128)(2,1)} %all-gather.27.cloned.1.call-done, bf16[2048,4096]{1,0:T(8,128)(2,1)} %constant_dynamic-update-slice_fusion, ...), kind=kOutput, calls=%fused_computation.1 | convolution fusion | flops 23127719936 | bytes 70385664 | tf_op jit(solution)/shard_map/dot_general | solution.py:23
  1316.0 280.4 %reduce-scatter.16.cloned.1.call-done = f32[256,4096]{1,0:T(8,128)} async-done(((f32[1024,4096]{1,0:T(8,128)}), f32[256,4096]{1,0:T(8,128)}) %reduce-scatter.16.cloned.1.call-update) | async-done | bytes 4194320 | tf_op jit(solution)/shard_map/reduce_scatter | solution.py:190
  1608.6 149.5 %all-gather.29.cloned.1.call-done = bf16[1024,4096]{1,0:T(8,128)(2,1)} async-done(((bf16[256,4096]{1,0:T(8,128)(2,1)}), bf16[1024,4096]{1,0:T(8,128)(2,1)}) %all-gather.29.cloned.1.call-update) | async-done | bytes 8388624 | tf_op jit(solution)/shard_map/all_gather | solution.py:196
  2106.2 86.8 %reduce-scatter.18.cloned.1.call-done = f32[256,4096]{1,0:T(8,128)} async-done(((f32[1024,4096]{1,0:T(8,128)}), f32[256,4096]{1,0:T(8,128)}) %reduce-scatter.18.cloned.1.call-update) | async-done | bytes 4194320 | tf_op jit(solution)/shard_map/reduce_scatter | solution.py:252
  2196.5 46.8 %all-reduce.2 = (f32[4096]{0:T(1024)}, f32[4096]{0:T(1024)}) all-reduce(f32[4096]{0:T(1024)S(1)} %get-tuple-element.125, f32[4096]{0:T(1024)S(1)} %copy-done.77), channel_id=1, replica_groups=mesh['dp'=8,'tensor'=4] {'dp','tensor'}, use_global_device_ids=true, to_apply=%region_21.22 | all-reduce | flops 8192 | bytes 65536 | tf_op jit(solution)/shard_map/psum | solution.py:269
  2243.3 98.3 %reduce-scatter.14.cloned.1.call-done = bf16[256,4096]{1,0:T(8,128)(2,1)} async-done(((bf16[1024,4096]{1,0:T(8,128)(2,1)}), bf16[256,4096]{1,0:T(8,128)(2,1)}) %reduce-scatter.14.cloned.1.call-update) | async-done | bytes 2097168 | tf_op jit(solution)/shard_map/reduce_scatter | solution.py:166
  2350.3 255.4 %reduce-scatter.28.cloned.1.call-done = f32[512,2752]{0,1:T(8,128)} async-done(((f32[4096,2752]{0,1:T(8,128)}), f32[512,2752]{0,1:T(8,128)}) %reduce-scatter.28.cloned.1.call-update) | async-done | bytes 5636112 | tf_op jit(solution)/shard_map/reduce_scatter | solution.py:265
  2605.7 263.5 %reduce-scatter.30.cloned.1.call-done = f32[512,2752]{0,1:T(8,128)} async-done(((f32[4096,2752]{0,1:T(8,128)}), f32[512,2752]{0,1:T(8,128)}) %reduce-scatter.30.cloned.1.call-update) | async-done | bytes 5636112 | tf_op jit(solution)/shard_map/reduce_scatter | solution.py:266
  2869.1 263.4 %reduce-scatter.32.cloned.1.call-done = f32[2752,512]{1,0:T(8,128)} async-done(((f32[2752,4096]{1,0:T(8,128)}), f32[2752,512]{1,0:T(8,128)}) %reduce-scatter.32.cloned.1.call-update) | async-done | bytes 5636112 | tf_op jit(solution)/shard_map/reduce_scatter | solution.py:267
  3132.6 120.4 %reduce-scatter.20.cloned.1.call-done = f32[512,1024]{1,0:T(8,128)} async-done(((f32[4096,1024]{1,0:T(8,128)}), f32[512,1024]{1,0:T(8,128)}) %reduce-scatter.20.cloned.1.call-update) | async-done | bytes 2097168 | tf_op jit(solution)/shard_map/reduce_scatter | solution.py:261
  3253.0 120.6 %reduce-scatter.22.cloned.1.call-done = f32[512,1024]{1,0:T(8,128)} async-done(((f32[4096,1024]{1,0:T(8,128)}), f32[512,1024]{1,0:T(8,128)}) %reduce-scatter.22.cloned.1.call-update) | async-done | bytes 2097168 | tf_op jit(solution)/shard_map/reduce_scatter | solution.py:262
  3373.5 120.4 %reduce-scatter.24.cloned.1.call-done = f32[512,1024]{1,0:T(8,128)} async-done(((f32[4096,1024]{1,0:T(8,128)}), f32[512,1024]{1,0:T(8,128)}) %reduce-scatter.24.cloned.1.call-update) | async-done | bytes 2097168 | tf_op jit(solution)/shard_map/reduce_scatter | solution.py:263
  3493.9 120.6 %reduce-scatter.26.cloned.1.call-done = f32[1024,512]{1,0:T(8,128)} async-done(((f32[1024,4096]{1,0:T(8,128)}), f32[1024,512]{1,0:T(8,128)}) %reduce-scatter.26.cloned.1.call-update) | async-done | bytes 2097168 | tf_op jit(solution)/shard_map/reduce_scatter | solution.py:264
  (372 shorter events, 650.1 us)
Async XLA Ops:
  7.2 158.8 %all-gather.11.cloned.1.call-start = ((), (), s32[]{:S(2)}) async-start(), calls=%async_computation.11 | async-start | bytes 10485760 | tf_op jit(solution)/shard_map/all_gather | solution.py:101
  13.5 207.0 %all-gather.13.cloned.1.call-start = ((), (), s32[]{:S(2)}) async-start(), calls=%async_computation.12 | async-start | bytes 9437184 | tf_op jit(solution)/shard_map/all_gather | solution.py:90
  14.2 262.6 %all-gather.15.cloned.1.call-start = ((), (), s32[]{:S(2)}) async-start(), calls=%async_computation.13 | async-start | bytes 9437184 | tf_op jit(solution)/shard_map/all_gather | solution.py:88
  15.0 318.0 %all-gather.17.cloned.1.call-start = ((), (), s32[]{:S(2)}) async-start(), calls=%async_computation.14 | async-start | bytes 9437184 | tf_op jit(solution)/shard_map/all_gather | solution.py:89
  15.6 375.2 %all-gather.19.cloned.1.call-start = ((), (), s32[]{:S(2)}) async-start(), calls=%async_computation.15 | async-start | bytes 9437184 | tf_op jit(solution)/shard_map/all_gather | solution.py:91
  16.1 669.9 %reduce-scatter.12.cloned.1.call-start = ((), (), s32[]{:S(2)}) async-start(), calls=%async_computation.16 | async-start | bytes 20971520 | tf_op jit(solution)/shard_map/reduce_scatter | solution.py:153
  405.6 475.7 %all-gather.23.cloned.1.call-start = ((), (), s32[]{:S(2)}) async-start(), calls=%async_computation.18 | async-start | bytes 25362432 | tf_op jit(solution)/shard_map/all_gather | solution.py:94
  406.4 570.4 %all-gather.21.cloned.1.call-start = ((), (), s32[]{:S(2)}) async-start(), calls=%async_computation.17 | async-start | bytes 10485760 | tf_op jit(solution)/shard_map/all_gather | solution.py:158
  692.8 402.8 %all-gather.25.cloned.1.call-start = ((), (), s32[]{:S(2)}) async-start(), calls=%async_computation.19 | async-start | bytes 25362432 | tf_op jit(solution)/shard_map/all_gather | solution.py:95
  693.5 522.7 %all-gather.27.cloned.1.call-start = ((), (), s32[]{:S(2)}) async-start(), calls=%async_computation.20 | async-start | bytes 25362432 | tf_op jit(solution)/shard_map/all_gather | solution.py:96
  694.1 902.3 %reduce-scatter.16.cloned.1.call-start = ((), (), s32[]{:S(2)}) async-start(), calls=%async_computation.22 | async-start | bytes 20971520 | tf_op jit(solution)/shard_map/reduce_scatter | solution.py:190
  695.1 49.1 %collective-permute-start = (bf16[256,4096]{1,0:T(8,128)(2,1)S(1)}, bf16[256,4096]{1,0:T(8,128)(2,1)S(1)}, u32[]{:S(2)}, u32[]{:S(2)}) collective-permute-start(bf16[256,4096]{1,0:T(8,128)(2,1)S(1)} %broadcast_multiply_fusion.1), channel_id=1, source_target_pairs={{0,1},{1,2},{2,3},{3,0},{4,5},{5,6},{6,7},{7,4},{8,9},{9,10},{10,1... | collective-permute-start | bytes 6291464 | tf_op jit(solution)/shard_map/ppermute | solution.py:176
  745.5 48.2 %collective-permute-start.1 = (bf16[256,4096]{1,0:T(8,128)(2,1)S(1)}, bf16[256,4096]{1,0:T(8,128)(2,1)}, u32[]{:S(2)}, u32[]{:S(2)}) collective-permute-start(bf16[256,4096]{1,0:T(8,128)(2,1)S(1)} %collective-permute-done), channel_id=1, source_target_pairs={{0,1},{1,2},{2,3},{3,0},{4,5},{5,6},{6,7},{7,4},{8,9},{9,10},{10,1... | collective-permute-start | bytes 6291464 | tf_op jit(solution)/shard_map/ppermute | solution.py:176
  793.7 68.0 %collective-permute-start.2 = (bf16[256,4096]{1,0:T(8,128)(2,1)}, bf16[256,4096]{1,0:T(8,128)(2,1)}, u32[]{:S(2)}, u32[]{:S(2)}) collective-permute-start(bf16[256,4096]{1,0:T(8,128)(2,1)} %collective-permute-done.1), channel_id=1, source_target_pairs={{0,1},{1,2},{2,3},{3,0},{4,5},{5,6},{6,7},{7,4},{8,9},{9,10},{10,1... | collective-permute-start | bytes 6291464 | tf_op jit(solution)/shard_map/ppermute | solution.py:176
  1316.0 442.1 %all-gather.29.cloned.1.call-start = ((), (), s32[]{:S(2)}) async-start(), calls=%async_computation.23 | async-start | bytes 10485760 | tf_op jit(solution)/shard_map/all_gather | solution.py:196
  1607.5 585.5 %reduce-scatter.18.cloned.1.call-start = ((), (), s32[]{:S(2)}) async-start(), calls=%async_computation.24 | async-start | bytes 20971520 | tf_op jit(solution)/shard_map/reduce_scatter | solution.py:252
  1914.3 427.2 %reduce-scatter.14.cloned.1.call-start = ((), (), s32[]{:S(2)}) async-start(), calls=%async_computation.21 | async-start | bytes 10485760 | tf_op jit(solution)/shard_map/reduce_scatter | solution.py:166
  1945.2 660.5 %reduce-scatter.28.cloned.1.call-start = ((), (), s32[]{:S(2)}) async-start(), calls=%async_computation.29 | async-start | bytes 50724864 | tf_op jit(solution)/shard_map/reduce_scatter | solution.py:265
  1977.1 892.1 %reduce-scatter.30.cloned.1.call-start = ((), (), s32[]{:S(2)}) async-start(), calls=%async_computation.30 | async-start | bytes 50724864 | tf_op jit(solution)/shard_map/reduce_scatter | solution.py:266
  2008.9 1123.7 %reduce-scatter.32.cloned.1.call-start = ((), (), s32[]{:S(2)}) async-start(), calls=%async_computation.31 | async-start | bytes 50724864 | tf_op jit(solution)/shard_map/reduce_scatter | solution.py:267
  2040.8 1212.2 %reduce-scatter.20.cloned.1.call-start = ((), (), s32[]{:S(2)}) async-start(), calls=%async_computation.25 | async-start | bytes 18874368 | tf_op jit(solution)/shard_map/reduce_scatter | solution.py:261
  2057.1 1316.4 %reduce-scatter.22.cloned.1.call-start = ((), (), s32[]{:S(2)}) async-start(), calls=%async_computation.26 | async-start | bytes 18874368 | tf_op jit(solution)/shard_map/reduce_scatter | solution.py:262
  2073.6 1420.4 %reduce-scatter.24.cloned.1.call-start = ((), (), s32[]{:S(2)}) async-start(), calls=%async_computation.27 | async-start | bytes 18874368 | tf_op jit(solution)/shard_map/reduce_scatter | solution.py:263
  2089.9 1524.6 %reduce-scatter.26.cloned.1.call-start = ((), (), s32[]{:S(2)}) async-start(), calls=%async_computation.28 | async-start | bytes 18874368 | tf_op jit(solution)/shard_map/reduce_scatter | solution.py:264
  (103 other events, 5087.2 us)
Sparse Core Ops, SparseCore 0:
  13.6 152.3 all-gather.10
  167.9 52.6 all-gather.12
  222.4 54.3 all-gather.14
  278.6 54.3 all-gather.16
  334.7 55.9 all-gather.18
  405.7 280.3 reduce-scatter.11
  688.1 119.3 all-gather.22
  809.7 166.9 all-gather.20
  978.8 116.8 all-gather.24
  1097.5 118.6 all-gather.26
  1316.1 280.2 reduce-scatter.15
  1607.6 150.3 all-gather.28
  1914.4 278.5 reduce-scatter.17
  2195.3 146.1 reduce-scatter.13
  2346.2 259.4 reduce-scatter.27
  2610.3 258.7 reduce-scatter.29
  2873.7 258.7 reduce-scatter.31
  3137.0 115.9 reduce-scatter.19
  3257.5 115.9 reduce-scatter.21
  3377.9 115.9 reduce-scatter.23
  3498.5 115.9 reduce-scatter.25
